TPU v7x, 32 devices: a whole 2x2x4 slice. The times are simulated.
32 devices in a mesh: wide: 8 (over z, core), narrow: 4 (over y, x).
Axes of the slice: x: 2, y: 2, z: 4, core: 2. Of those that a mesh axis runs over, the one named last changes fastest.
Arguments:
- tokens: bfloat16 [8192, 2048], P('wide'), may hold values from -4 to 4
- cotangent: bfloat16 [8192, 2048], P('wide'), may hold values from -4 to 4
- noise_emb: float32 [128, 2048], P('wide'), may hold values from -2.5 to 2.5
- offsets: int32 [8, 16], P('wide'), may hold values from 0 to 1024, as said below
- lengths: int32 [8, 16], P('wide'), may hold values from 0 to 1024, as said below
- group_ids: int32 [8, 16], P('wide'), may hold values from 0 to 2, as said below
- group_table: float32 [3, 2048], replicated, may hold values from -2.5 to 2.5
- w_qkv: bfloat16 [3, 2048, 2048], P(None, None, 'narrow'), may hold values from -0.125 to 0.125
- w_out: bfloat16 [2048, 2048], P('narrow'), may hold values from -0.5 to 0.5
- w_up: bfloat16 [2048, 8192], P(None, 'narrow'), may hold values from -0.125 to 0.125
- b_up: float32 [8192], P('narrow'), may hold values from -2.5 to 2.5
- w_down: bfloat16 [8192, 2048], P('narrow'), may hold values from -0.09375 to 0.09375
- w_mod: bfloat16 [2048, 6, 2048], P(None, None, 'narrow'), may hold values from -0.0625 to 0.0625
- b_mod: float32 [6, 2048], P(None, 'narrow'), may hold values from -1.5 to 1.5
Outputs:
- result: bfloat16 [8192, 2048], P('wide')
- grad_tokens: bfloat16 [8192, 2048], P('wide')
- grad_noise: float32 [128, 2048], P('wide')
- grad_group_table: float32 [3, 2048], P(None, 'wide')
- grad_w_qkv: float32 [3, 2048, 2048], P(None, 'wide', 'narrow')
- grad_w_out: float32 [2048, 2048], P('narrow', 'wide')
- grad_w_up: float32 [2048, 8192], P('wide', 'narrow')
- grad_b_up: float32 [8192], P(('narrow', 'wide'))
- grad_w_down: float32 [8192, 2048], P('narrow', 'wide')
- grad_w_mod: float32 [2048, 6, 2048], P('wide', None, 'narrow')
- grad_b_mod: float32 [6, 2048], P(None, ('narrow', 'wide'))
Inputs may be any that keep to these rules, and one draw needn't show every extreme that they name: `offsets`: each index of wide holds images of one length, 1024, 256 or 64 tokens, laid end to end from token 0 and filling its 1024 tokens: slot s starts at s times that length. Slots past the last image start at 1024. Every length occurs on some index of wide. `lengths`: the length of each image slot; 0 for slots past the last image of an index of wide. `group_ids`: 0 on indices of wide with images of 1024 tokens, 1 with 256, 2 with 64, for all slots of that index; every group occurs.
All inputs are finite; a program needn't handle non-finite values.
Results may differ from a plain program's by a relative error of at most 0.018.
Values may be sent and summed in bfloat16 or wider, within the bound.
No kernel may reach another device: no remote copies, remote signals or barrier semaphores. Data moves between devices by JAX's collectives and lax.ppermute only.
A program may use at most 320 MiB of HBM per device.

v0:
```python
import jax
import jax.numpy as jnp
from jax import lax
from jax.sharding import PartitionSpec as P

HEAD_DIM = 128


highest = lax.Precision.HIGHEST


def normalize(values):
    centred = values - jnp.mean(values, axis=-1, keepdims=True)
    recip = lax.rsqrt(jnp.mean(centred * centred, axis=-1, keepdims=True) + 1e-06)
    return (centred * recip, recip)


def norm_back(grad, normed, recip):
    first = jnp.mean(grad, axis=-1, keepdims=True)
    second = jnp.mean(grad * normed, axis=-1, keepdims=True)
    return recip * (grad - first - normed * second)


def gelu_slope(values):
    cumul = 0.5 * (1.0 + lax.erf(values * 0.7071067811865476))
    density = jnp.exp(-0.5 * values * values) * 0.3989422804014327
    return cumul + values * density


def body(
    tokens,
    cotangent,
    noise_emb,
    offsets,
    lengths,
    group_ids,
    group_table,
    w_qkv,
    w_out,
    w_up,
    b_up,
    w_down,
    w_mod,
    b_mod,
):
    f32 = jnp.float32
    half = jnp.bfloat16
    tok_dev, width = tokens.shape
    slots = offsets.shape[1]
    local_width = w_qkv.shape[2]
    heads_here = local_width // HEAD_DIM
    groups = group_table.shape[0]
    positions = jnp.arange(tok_dev, dtype=jnp.int32)[:, None]
    member = ((positions >= offsets) & (positions < offsets + lengths)).astype(f32)
    image_of = jnp.dot(member, jnp.arange(slots, dtype=f32), precision=highest)
    group_hot = (group_ids[0][:, None] == jnp.arange(groups, dtype=jnp.int32)[None, :]).astype(f32)
    cond = noise_emb + jnp.dot(group_hot, group_table, precision=highest)
    silu_low = jax.nn.silu(cond).astype(half)
    mod_local = jnp.dot(
        silu_low, w_mod.reshape(width, 6 * local_width), preferred_element_type=f32
    ) + b_mod.reshape(6 * local_width)
    mod_full = lax.all_gather(
        mod_local.reshape(slots, 6, local_width), "narrow", axis=2, tiled=True
    )

    def per_token(column):
        return jnp.dot(member, mod_full[:, column], precision=highest)

    shift_a = per_token(0)
    scale_a = per_token(1)
    gate_a = per_token(2)
    shift_b = per_token(3)
    scale_b = per_token(4)
    gate_b = per_token(5)
    tok_f = tokens.astype(f32)
    normed_a, recip_a = normalize(tok_f)
    mixed_a = (normed_a * (1.0 + scale_a) + shift_a).astype(half)
    factor = HEAD_DIM ** (-0.5)
    query = (jnp.dot(mixed_a, w_qkv[0], preferred_element_type=f32) * factor).astype(half)
    keys = jnp.dot(mixed_a, w_qkv[1], preferred_element_type=f32).astype(half)
    values = jnp.dot(mixed_a, w_qkv[2], preferred_element_type=f32).astype(half)
    block_rows = min(512, tok_dev)
    blocks = tok_dev // block_rows
    q_blocks = query.reshape(blocks, block_rows, heads_here, HEAD_DIM)
    key_heads = keys.reshape(tok_dev, heads_here, HEAD_DIM)
    value_heads = values.reshape(tok_dev, heads_here, HEAD_DIM)
    image_blocks = image_of.reshape(blocks, block_rows)

    def block_scores(q_block, image_block):
        scores = jnp.einsum("qhd,khd->hqk", q_block, key_heads, preferred_element_type=f32)
        same = image_block[:, None] == image_of[None, :]
        return jnp.where(same[None], scores, -1e30)

    def forward_block(item):
        scores = block_scores(item[0], item[1])
        top = jnp.max(scores, axis=-1, keepdims=True)
        expo = jnp.exp(scores - top)
        total = jnp.sum(expo, axis=-1, keepdims=True)
        probs = expo / total
        out = jnp.einsum(
            "hqk,khd->qhd", probs.astype(half), value_heads, preferred_element_type=f32
        )
        return (out.astype(half), (top + jnp.log(total))[..., 0])

    outs, log_totals = lax.map(forward_block, (q_blocks, image_blocks))
    heads_out = outs.reshape(tok_dev, local_width)
    attended = lax.psum(jnp.dot(heads_out, w_out, preferred_element_type=f32), "narrow")
    middle = tok_f + gate_a * attended
    normed_b, recip_b = normalize(middle)
    mixed_b = (normed_b * (1.0 + scale_b) + shift_b).astype(half)
    hidden_pre = jnp.dot(mixed_b, w_up, preferred_element_type=f32) + b_up
    hidden = jax.nn.gelu(hidden_pre, approximate=False).astype(half)
    mlp_out = lax.psum(
        jnp.dot(hidden, w_down, preferred_element_type=f32).astype(jnp.bfloat16), "narrow"
    ).astype(jnp.float32)
    result = (middle + gate_b * mlp_out).astype(half)
    grad_out = cotangent.astype(f32)
    d_mlp = (grad_out * gate_b).astype(half)
    d_hidden = jnp.dot(d_mlp, w_down.T, preferred_element_type=f32).astype(half)
    d_pre = (d_hidden.astype(f32) * gelu_slope(hidden_pre)).astype(half)
    grad_b_up = jnp.sum(d_pre.astype(f32), axis=0)
    grad_w_down = jnp.dot(hidden.T, d_mlp, preferred_element_type=f32)
    grad_w_up = jnp.dot(mixed_b.T, d_pre, preferred_element_type=f32)
    d_mixed_b = lax.psum(jnp.dot(d_pre, w_up.T, preferred_element_type=f32), "narrow")
    d_middle = grad_out + norm_back(d_mixed_b * (1.0 + scale_b), normed_b, recip_b)
    d_attn = (d_middle * gate_a).astype(half)
    grad_w_out = jnp.dot(heads_out.T, d_attn, preferred_element_type=f32)
    d_heads = jnp.dot(d_attn, w_out.T, preferred_element_type=f32).astype(half)
    d_blocks = d_heads.reshape(blocks, block_rows, heads_here, HEAD_DIM)

    def backward_block(carry, item):
        grad_key, grad_value = carry
        q_block, image_block, d_block, lse_block = item
        probs = jnp.exp(block_scores(q_block, image_block) - lse_block[..., None])
        d_probs = jnp.einsum("qhd,khd->hqk", d_block, value_heads, preferred_element_type=f32)
        inner = jnp.sum(probs * d_probs, axis=-1, keepdims=True)
        d_scores = (probs * (d_probs - inner)).astype(half)
        grad_query = jnp.einsum("hqk,khd->qhd", d_scores, key_heads, preferred_element_type=f32)
        grad_key = grad_key + jnp.einsum(
            "hqk,qhd->khd", d_scores, q_block, preferred_element_type=f32
        )
        grad_value = grad_value + jnp.einsum(
            "hqk,qhd->khd", probs.astype(half), d_block, preferred_element_type=f32
        )
        return ((grad_key, grad_value), grad_query)

    zeros = jnp.zeros((tok_dev, heads_here, HEAD_DIM), f32)
    (grad_key, grad_value), grad_query = lax.scan(
        backward_block, (zeros, zeros), (q_blocks, image_blocks, d_blocks, log_totals)
    )
    d_query = (grad_query.reshape(tok_dev, local_width) * factor).astype(half)
    d_key = grad_key.reshape(tok_dev, local_width).astype(half)
    d_value = grad_value.reshape(tok_dev, local_width).astype(half)
    d_proj = jnp.stack([d_query, d_key, d_value], axis=1)
    grad_w_qkv = jnp.einsum("td,tiv->idv", mixed_a, d_proj, preferred_element_type=f32)
    d_mixed_a = lax.psum(
        jnp.einsum("tiv,idv->td", d_proj, w_qkv, preferred_element_type=f32).astype(jnp.bfloat16),
        "narrow",
    ).astype(jnp.float32)
    grad_tokens = (d_middle + norm_back(d_mixed_a * (1.0 + scale_a), normed_a, recip_a)).astype(
        half
    )
    start = lax.axis_index("narrow") * local_width

    def own(values_in):
        return lax.dynamic_slice_in_dim(values_in, start, local_width, 1)

    token_terms = jnp.stack(
        [
            own(d_mixed_a),
            own(d_mixed_a * normed_a),
            own(d_middle * attended),
            own(d_mixed_b),
            own(d_mixed_b * normed_b),
            own(grad_out * mlp_out),
        ],
        axis=1,
    )
    d_modes = jnp.einsum("ts,tcv->scv", member, token_terms, precision=highest).astype(half)
    flat_modes = d_modes.reshape(slots, 6 * local_width)
    d_silu = lax.psum(
        jnp.dot(
            flat_modes, w_mod.reshape(width, 6 * local_width).T, preferred_element_type=f32
        ).astype(jnp.bfloat16),
        "narrow",
    ).astype(jnp.float32)
    sigma = jax.nn.sigmoid(cond)
    grad_noise = d_silu * sigma * (1.0 + cond * (1.0 - sigma))
    grad_table = jnp.dot(group_hot.T, grad_noise, precision=highest)
    grad_b_mod = jnp.sum(d_modes.astype(f32), axis=0)
    grad_w_mod = jnp.dot(silu_low.T, flat_modes, preferred_element_type=f32).reshape(
        width, 6, local_width
    )
    summed = (
        lax.psum_scatter(
            grad_w_qkv.astype(jnp.bfloat16), "wide", scatter_dimension=1, tiled=True
        ).astype(jnp.float32),
        lax.psum_scatter(
            grad_w_out.astype(jnp.bfloat16), "wide", scatter_dimension=1, tiled=True
        ).astype(jnp.float32),
        lax.psum_scatter(
            grad_w_up.astype(jnp.bfloat16), "wide", scatter_dimension=0, tiled=True
        ).astype(jnp.float32),
        lax.psum_scatter(
            grad_b_up.astype(jnp.bfloat16), "wide", scatter_dimension=0, tiled=True
        ).astype(jnp.float32),
        lax.psum_scatter(
            grad_w_down.astype(jnp.bfloat16), "wide", scatter_dimension=1, tiled=True
        ).astype(jnp.float32),
        lax.psum_scatter(
            grad_w_mod.astype(jnp.bfloat16), "wide", scatter_dimension=0, tiled=True
        ).astype(jnp.float32),
        lax.psum_scatter(
            grad_b_mod.astype(jnp.bfloat16), "wide", scatter_dimension=1, tiled=True
        ).astype(jnp.float32),
        lax.psum_scatter(
            grad_table.astype(jnp.bfloat16), "wide", scatter_dimension=1, tiled=True
        ).astype(jnp.float32),
    )
    return (
        result,
        grad_tokens,
        grad_noise,
        summed[7],
        summed[0],
        summed[1],
        summed[2],
        summed[3],
        summed[4],
        summed[5],
        summed[6],
    )


def solution(mesh):
    in_specs = (
        P("wide", None),
        P("wide", None),
        P("wide", None),
        P("wide", None),
        P("wide", None),
        P("wide", None),
        P(),
        P(None, None, "narrow"),
        P("narrow", None),
        P(None, "narrow"),
        P("narrow"),
        P("narrow", None),
        P(None, None, "narrow"),
        P(None, "narrow"),
    )
    out_specs = (
        P("wide", None),
        P("wide", None),
        P("wide", None),
        P(None, "wide"),
        P(None, "wide", "narrow"),
        P("narrow", "wide"),
        P("wide", "narrow"),
        P(("narrow", "wide")),
        P("narrow", "wide"),
        P("wide", None, "narrow"),
        P(None, ("narrow", "wide")),
    )
    return jax.shard_map(body, mesh=mesh, in_specs=in_specs, out_specs=out_specs, check_vma=False)
```

profile of v0, /device:TPU:0, one launch (start us, length us, event | category | flops | bytes accessed | tf_op | source)
XLA Modules:
  0.0 1386.1 jit_solution(8295451466740319210)
XLA Ops:
  13.7 17.1 %copy.59 = bf16[2048,6,512]{0,2,1:T(8,128)(2,1)} copy(bf16[2048,6,512]{2,0,1:T(8,128)(2,1)} %param.30) | data formatting | bytes 25165824 | tf_op args[12]
  39.8 15.2 %all_gather.3 = f32[16,6,2048]{2,1,0:T(8,128)S(1)} all-gather(f32[16,6,512]{2,1,0:T(8,128)S(1)} %reshape.223), channel_id=1, replica_groups=mesh['wide'=8,'narrow'=4] {'narrow'}, dimensions={2}, use_global_device_ids=true | all-gather | bytes 983040 | tf_op jit(solution)/shard_map/all_gather | solution.py:62
  82.9 19.1 %while.27 = (s32[]{:T(128)}, bf16[2,512,4,128]{3,2,1,0:T(4,128)(2,1)}, f32[2,4,512]{2,1,0:T(4,128)}, f32[2,512]{1,0:T(2,128)S(1)}, f32[1024]{0:T(1024)S(1)}, /*i...) while((s32[]{:T(128)}, ...), condition=%wide.region_5.6_spmd, body=%wide.region_2.5_spmd.sunk | while | flops 1093400576 | bytes 44247296 | solution.py:105
  122.6 159.3 %all-reduce.7.cloned.1.call-done = f32[1024,2048]{1,0:T(8,128)} async-done(((f32[1024,2048]{1,0:T(8,128)}), f32[1024,2048]{1,0:T(8,128)}) %all-reduce.7.cloned.1.call-update) | async-done | bytes 8388624 | tf_op jit(solution)/shard_map/psum | solution.py:107
  307.9 31.0 %fusion.32 = (bf16[1024,2048]{1,0:T(8,128)(2,1)}, f32[1024,2048]{1,0:T(8,128)}) fusion(f32[2048]{0:T(1024)S(1)} %copy-done.53, bf16[1024,2048]{1,0:T(8,128)(2,1)S(1)} %add_convert_fusion.2, bf16[2048,2048]{1,0:T(8,128)(2,1)} %param.27), kind=kOutput, calls=%fused_computation.52 | convolution fusion | flops 8728346624 | bytes 25174016 | tf_op jit(solution)/shard_map/dot_general | solution.py:111
  338.9 20.5 %fusion.117 = (bf16[2048]{0:T(1024)(128)(2,1)}, bf16[1024,2048]{1,0:T(8,128)(2,1)}) fusion(f32[1024,2048]{1,0:T(8,128)} %get-tuple-element.305, f32[2048]{0:T(1024)S(1)} %copy-done.53, bf16[2048,2048]{1,0:T(8,128)(2,1)} %param.29, f32[1024,2048]{1,0:T(8,128)} %fusion.84, bf16[1024,2048]{1,0:T(8,128)(2,1)} %param.19), kind=kOutput, calls=%fused_computation.182 | convolution fusion | flops 8625584128 | bytes 33566720 | tf_op jit(solution)/shard_map/dot_general | solution.py:119
  359.4 14.9 %fusion.119 = f32[1024,2048]{1,0:T(8,128)} fusion(bf16[1024,2048]{1,0:T(8,128)(2,1)} %get-tuple-element.307, bf16[2048,2048]{1,0:T(8,128)(2,1)} %param.27), kind=kOutput, calls=%fused_computation.185 | convolution fusion | flops 8589934592 | bytes 20971520 | tf_op jit(solution)/shard_map/dot_general | solution.py:124
  374.4 13.8 convolution_convert_fusion.3
  388.2 159.1 %all-reduce.9.cloned.1.call-done = f32[1024,2048]{1,0:T(8,128)} async-done(((f32[1024,2048]{1,0:T(8,128)}), f32[1024,2048]{1,0:T(8,128)}) %all-reduce.9.cloned.1.call-update) | async-done | bytes 8388624 | tf_op jit(solution)/shard_map/psum | solution.py:124
  556.8 18.6 %multiply_convert_fusion.1 = (bf16[1024,2048]{1,0:T(8,128)(2,1)}, f32[1024,2048]{1,0:T(8,128)}) fusion(f32[1024,2048]{1,0:T(8,128)} %get-tuple-element.303, f32[1024]{0:T(1024)S(1)} %get-tuple-element.310, f32[1024]{0:T(1024)S(1)} %get-tuple-element.311, f32[1024,2048]{1,0:T(8,128)} %all-reduce.9.cloned.1.call-done, f32[1024,2048]{1,0:T(8,128)} %fusion.81, ...), kind=kLoop, calls=%fused_computation.62 | loop fusion | flops 25165824 | bytes 50348032 | tf_op jit(solution)/shard_map/convert_element_type | solution.py:126
  583.3 33.1 %while.28 = (s32[]{:T(128)}, f32[1024,4,128]{0,2,1:T(8,128)}, f32[1024,4,128]{0,2,1:T(8,128)}, f32[2,512,4,128]{3,1,2,0:T(8,128)}, bf16[2,512,4,128]{3,1,2,0:T(8...) while((s32[]{:T(128)}, f32[1024,4,128]{0,2,1:T(8,128)}, ...), condition=%wide.region_15.16_spmd.clone, body=%wide.region_13.15_spmd.clone.sunk | while | flops 2712139776 | bytes 139528592 | solution.py:148
  623.8 10.9 bitcast_convert_fusion
  641.6 166.5 %all-reduce.13.cloned.1.call-done = (bf16[1024,2048]{1,0:T(8,128)(2,1)}, bf16[1024,2048]{1,0:T(8,128)(2,1)}) async-done(((bf16[1024,2048]{1,0:T(8,128)(2,1)}, bf16[1024,2048]{1,0:T(8,128)(2,1)}), (bf16[1024,2048]{1,0:T(8,128)(2,1)}, bf16[1024,2048]{1,0:T(8,128)(2,1)})) %all-reduce.13.cloned.1.call-update) | async-done | bytes 8388624 | tf_op jit(solution)/shard_map/psum | solution.py:113
  857.3 14.5 %convolution_convert_fusion.1 = bf16[2048,2048]{1,0:T(8,128)(2,1)} fusion(bf16[1024,2048]{1,0:T(8,128)(2,1)} %copy-done.19, bf16[1024,2048]{1,0:T(8,128)(2,1)} %get-tuple-element.307), kind=kOutput, calls=%fused_computation.89 | convolution fusion | flops 8594128896 | bytes 16777216 | tf_op jit(solution)/shard_map/dot_general | solution.py:123
  871.9 15.3 %convolution_convert_fusion = bf16[2048,2048]{1,0:T(8,128)(2,1)} fusion(bf16[1024,2048]{1,0:T(8,128)(2,1)} %get-tuple-element.304, f32[1024,2048]{1,0:T(8,128)} %fusion.84, bf16[1024,2048]{1,0:T(8,128)(2,1)} %param.19), kind=kOutput, calls=%fused_computation.88 | convolution fusion | flops 8600420352 | bytes 25165824 | tf_op jit(solution)/shard_map/dot_general | solution.py:122
  896.0 11.3 convert_bitcast_fusion
  915.8 16.1 %all-reduce = bf16[2048]{0:T(1024)(128)(2,1)S(1)} all-reduce(bf16[2048]{0:T(1024)(128)(2,1)S(1)} %copy-done.47), channel_id=6, replica_groups=mesh['wide'=8,'narrow'=4] {'wide'}, use_global_device_ids=true, to_apply=%region_25.26.clone | all-reduce | flops 2048 | bytes 8192
  934.3 88.4 %reduce-scatter.16.cloned.1.call-done = bf16[256,2048]{1,0:T(8,128)(2,1)} async-done(((bf16[2048,2048]{1,0:T(8,128)(2,1)}), bf16[256,2048]{1,0:T(8,128)(2,1)}) %reduce-scatter.16.cloned.1.call-update) | async-done | bytes 1048592 | tf_op jit(solution)/shard_map/reduce_scatter | solution.py:201
  1025.5 87.5 %reduce-scatter.18.cloned.1.call-done = bf16[2048,256]{1,0:T(8,128)(2,1)} async-done(((bf16[2048,2048]{1,0:T(8,128)(2,1)}), bf16[2048,256]{1,0:T(8,128)(2,1)}) %reduce-scatter.18.cloned.1.call-update) | async-done | bytes 1048592 | tf_op jit(solution)/shard_map/reduce_scatter | solution.py:207
  1115.7 11.6 add_convert_fusion.1
  1127.2 12.2 add_convert_fusion
  1145.2 30.7 %reduce-scatter.22.cloned.1.call-done = bf16[256,3]{1,0:T(8,128)(2,1)} async-done(((bf16[2048,3]{1,0:T(8,128)(2,1)}), bf16[256,3]{1,0:T(8,128)(2,1)}) %reduce-scatter.22.cloned.1.call-update) | async-done | bytes 1552
  1177.4 68.6 %reduce-scatter.12.cloned.1.call-done = bf16[3,256,512]{1,2,0:T(8,128)(2,1)} async-done(((bf16[3,2048,512]{1,2,0:T(8,128)(2,1)}), bf16[3,256,512]{1,2,0:T(8,128)(2,1)}) %reduce-scatter.12.cloned.1.call-update) | async-done | bytes 786448 | tf_op jit(solution)/shard_map/reduce_scatter | solution.py:195
  1248.5 127.4 %reduce-scatter.20.cloned.1.call-done = bf16[256,6,512]{2,0,1:T(8,128)(2,1)} async-done(((bf16[2048,6,512]{2,0,1:T(8,128)(2,1)}), bf16[256,6,512]{2,0,1:T(8,128)(2,1)}) %reduce-scatter.20.cloned.1.call-update) | async-done | bytes 1572880 | tf_op jit(solution)/shard_map/reduce_scatter | solution.py:210
  (296 shorter events, 259.5 us)
Async XLA Ops:
  7.2 94.8 %copy-start = (bf16[512,2048]{1,0:T(8,128)(2,1)S(1)}, bf16[512,2048]{1,0:T(8,128)(2,1)}, u32[]{:S(2)}) copy-start(bf16[512,2048]{1,0:T(8,128)(2,1)} %param.26) | copy-start | bytes 6291460
  7.2 274.7 %all-reduce.7.cloned.1.call-start = ((), (), s32[]{:S(2)}) async-start(), calls=%async_computation.7 | async-start | bytes 16777216 | tf_op jit(solution)/shard_map/psum | solution.py:107
  10.2 49.9 %copy-start.37 = (f32[1024]{0:T(1024)}, f32[1024]{0:T(1024)S(1)}, u32[]{:S(2)}) copy-start(f32[1024]{0:T(1024)S(1)} %broadcast_multiply_fusion.5) | copy-start | bytes 12292
  13.7 46.5 %copy-start.39 = (f32[1024]{0:T(1024)}, f32[1024]{0:T(1024)S(1)}, u32[]{:S(2)}) copy-start(f32[1024]{0:T(1024)S(1)} %add_rsqrt_fusion.1) | copy-start | bytes 12292
  13.7 17.1 %copy-start.33 = (f32[16,2048]{1,0:T(8,128)S(1)}, f32[16,2048]{1,0:T(8,128)}, u32[]{:S(2)}) copy-start(f32[16,2048]{1,0:T(8,128)} %param.20) | copy-start | bytes 393220
  13.7 17.1 %copy-start.45 = (f32[3,2048]{1,0:T(4,128)S(1)}, f32[3,2048]{1,0:T(4,128)}, u32[]{:S(2)}) copy-start(f32[3,2048]{1,0:T(4,128)} %param.24) | copy-start | bytes 73732
  30.8 25.4 %copy-start.41 = (s32[1,16]{1,0:T(1,128)S(1)}, s32[1,16]{1,0:T(1,128)}, u32[]{:S(2)}) copy-start(s32[1,16]{1,0:T(1,128)} %param.21) | copy-start | bytes 196
  30.8 25.4 %copy-start.54 = (s32[1,16]{1,0:T(1,128)S(1)}, s32[1,16]{1,0:T(1,128)}, u32[]{:S(2)}) copy-start(s32[1,16]{1,0:T(1,128)} %param.22) | copy-start | bytes 196
  39.8 20.4 %copy-start.7 = (bf16[1024,2048]{1,0:T(8,128)(2,1)S(1)}, bf16[1024,2048]{1,0:T(8,128)(2,1)}, u32[]{:S(2)}) copy-start(bf16[1024,2048]{1,0:T(8,128)(2,1)} %param.18) | copy-start | bytes 12582916
  56.3 243.7 %copy-start.43 = (s32[16]{0:T(128)}, s32[16]{0:T(128)S(1)}, u32[]{:S(2)}) copy-start(s32[16]{0:T(128)S(1)} %add_bitcast_fusion) | copy-start | bytes 196
  109.4 437.9 %all-reduce.9.cloned.1.call-start = ((), (), s32[]{:S(2)}) async-start(), calls=%async_computation.8 | async-start | bytes 16777216 | tf_op jit(solution)/shard_map/psum | solution.py:124
  307.9 31.0 %copy-start.19 = (bf16[1024,2048]{1,0:T(8,128)(2,1)}, bf16[1024,2048]{1,0:T(8,128)(2,1)S(1)}, u32[]{:S(2)}) copy-start(bf16[1024,2048]{1,0:T(8,128)(2,1)S(1)} %add_convert_fusion.2) | copy-start | bytes 12582916
  374.3 433.8 %all-reduce.13.cloned.1.call-start = ((), (), s32[]{:S(2)}) async-start(), calls=%async_computation.17 | async-start | bytes 16777216 | tf_op jit(solution)/shard_map/psum | solution.py:113
  634.7 259.0 %all-reduce.11.cloned.1.call-start = ((), (), s32[]{:S(2)}) async-start(), calls=%async_computation.9 | async-start | bytes 131072 | tf_op jit(solution)/shard_map/psum | solution.py:181
  641.6 169.8 %copy-start.38 = (f32[1024]{0:T(1024)S(1)}, f32[1024]{0:T(1024)}, u32[]{:S(2)}) copy-start(f32[1024]{0:T(1024)} %copy-done.37) | copy-start | bytes 12292
  641.6 169.9 %copy-start.40 = (f32[1024]{0:T(1024)S(1)}, f32[1024]{0:T(1024)}, u32[]{:S(2)}) copy-start(f32[1024]{0:T(1024)} %copy-done.39) | copy-start | bytes 12292
  851.3 81.2 %reduce-scatter.14.cloned.1.call-start = ((), (), s32[]{:S(2)}) async-start(), calls=%async_computation.11 | async-start | bytes 2359296 | tf_op jit(solution)/shard_map/reduce_scatter | solution.py:198
  857.3 165.4 %reduce-scatter.16.cloned.1.call-start = ((), (), s32[]{:S(2)}) async-start(), calls=%async_computation.12 | async-start | bytes 9437184 | tf_op jit(solution)/shard_map/reduce_scatter | solution.py:201
  871.8 241.1 %reduce-scatter.18.cloned.1.call-start = ((), (), s32[]{:S(2)}) async-start(), calls=%async_computation.13 | async-start | bytes 9437184 | tf_op jit(solution)/shard_map/reduce_scatter | solution.py:207
  887.3 256.5 %reduce-scatter.24.cloned.1.call-start = ((), (), s32[]{:S(2)}) async-start(), calls=%async_computation.16 | async-start | bytes 147456
  888.1 287.7 %reduce-scatter.22.cloned.1.call-start = ((), (), s32[]{:S(2)}) async-start(), calls=%async_computation.15 | async-start | bytes 589824
  896.0 350.0 %reduce-scatter.12.cloned.1.call-start = ((), (), s32[]{:S(2)}) async-start(), calls=%async_computation.10 | async-start | bytes 7077888 | tf_op jit(solution)/shard_map/reduce_scatter | solution.py:195
  907.3 468.6 %reduce-scatter.20.cloned.1.call-start = ((), (), s32[]{:S(2)}) async-start(), calls=%async_computation.14 | async-start | bytes 14155776 | tf_op jit(solution)/shard_map/reduce_scatter | solution.py:210
  1127.2 252.2 %copy-start.1 = (bf16[512,2048]{1,0:T(8,128)(2,1)S(1)}, bf16[512,2048]{1,0:T(8,128)(2,1)}, u32[]{:S(2)}) copy-start(bf16[512,2048]{1,0:T(8,128)(2,1)} %param.26) | copy-start | bytes 6291460
  (65 other events, 360.7 us)
Sparse Core Ops, SparseCore 0:
  109.5 172.3 all-reduce.6
  374.5 172.7 all-reduce.8
  634.8 173.2 all-reduce.12
  851.4 42.1 all-reduce.10
  896.4 35.7 reduce-scatter.13
  934.3 88.3 reduce-scatter.15
  1025.0 87.9 reduce-scatter.17
  1115.2 28.5 reduce-scatter.23
  1146.7 29.0 reduce-scatter.21
  1178.0 67.9 reduce-scatter.11
  1248.3 127.5 reduce-scatter.19
where the time goes:
time: 1390 us
  waiting for transfers between devices  897 us (65%)
  matrix products  258 us (19%)
  other arithmetic  126 us (9%)
  local copies, waits for them, and re-layouts  56.8 us (4%)
  blocking collectives  31.3 us (2%)
  between operations  15.4 us (1%)
    psum x1, waiting for transfers between devices, body(): lax.psum(jnp.dot(hidden, w_down, preferred_element_type=f32).astype(jnp.b...  166 us
    psum x1, waiting for transfers between devices, body(): lax.psum(jnp.dot(heads_out, w_out, preferred_element_type=f32), 'narrow')  159 us
    psum x1, waiting for transfers between devices, body(): lax.psum(jnp.dot(d_pre, w_up.T, preferred_element_type=f32), 'narrow')  159 us
    reduce_scatter x1, waiting for transfers between devices, body(): lax.psum_scatter(grad_w_mod.astype(jnp.bfloat16), 'wide', scatter_dimensi...  127 us
    reduce_scatter x1, waiting for transfers between devices, body(): lax.psum_scatter(grad_w_up.astype(jnp.bfloat16), 'wide', scatter_dimensio...  88.4 us
    reduce_scatter x1, waiting for transfers between devices, body(): lax.psum_scatter(grad_w_down.astype(jnp.bfloat16), 'wide', scatter_dimens...  87.5 us
    reduce_scatter x1, waiting for transfers between devices, body(): lax.psum_scatter(grad_w_qkv.astype(jnp.bfloat16), 'wide', scatter_dimensi...  68.6 us
    dot_general x6, matrix products, per_token(): return jnp.dot(member, mod_full[:, column], precision=highest)  39.6 us
  transfers between devices with their start and end apart: 11, of which 10 were waited for; matrix products, arithmetic and copies ran while one was open for 9% of the time, Pallas kernels for 0%

commit v1 on v0

v1 whole, which is shorter than its diff:
```python
import jax
import jax.numpy as jnp
from jax import lax
from jax.experimental import pallas as pl
from jax.experimental.pallas import tpu as pltpu
from jax.sharding import PartitionSpec as P

HEAD_DIM = 128
SPAN = 64
MASKED = -1e30

f32 = jnp.float32
half = jnp.bfloat16
highest = lax.Precision.HIGHEST
MIB = 1 << 20


def dot(left, right, dims):
    return lax.dot_general(left, right, (dims, ((), ())), preferred_element_type=f32)


def spec(shape, index):
    return pl.BlockSpec(shape, index)


def params(mib=56):
    return pltpu.CompilerParams(vmem_limit_bytes=mib * MIB)


def hop(values, distance, size):
    return lax.ppermute(values, "narrow", [(i, i ^ distance) for i in range(size)])


def spread(shard, size):
    if size != 4:
        return [shard] + [hop(shard, d, size) for d in range(1, size)]
    mid = shard.shape[0] // 2
    one = hop(shard, 1, size)
    two = hop(shard, 2, size)
    first = hop(two[:mid], 1, size)
    second = hop(one[mid:], 2, size)
    return [shard, one, two, jnp.concatenate([first, second], axis=0)]


def collect(chunks, size):
    own = chunks[0].astype(f32)
    if size != 4:
        for d in range(1, size):
            own = own + hop(chunks[d].astype(half), d, size).astype(f32)
        return own
    mid = chunks[0].shape[0] // 2
    far = chunks[3].astype(half)
    one = chunks[1]
    two = chunks[2]
    via_two = hop(far[:mid], 2, size)
    via_one = hop(far[mid:], 1, size)
    one = jnp.concatenate(
        [(one[:mid].astype(f32) + via_two.astype(f32)).astype(half), one[mid:].astype(half)], axis=0
    )
    two = jnp.concatenate(
        [two[:mid].astype(half), (two[mid:].astype(f32) + via_one.astype(f32)).astype(half)], axis=0
    )
    return own + hop(one, 1, size).astype(f32) + hop(two, 2, size).astype(f32)


def in_order(pieces, index, axis=0):
    step = pieces[0].shape[axis]
    shape = list(pieces[0].shape)
    shape[axis] = step * len(pieces)
    joined = jnp.zeros(shape, pieces[0].dtype)
    for d, piece in enumerate(pieces):
        joined = lax.dynamic_update_slice_in_dim(joined, piece, (index ^ d) * step, axis)
    return joined


def modes_kernel(silu_ref, w_ref, b_ref, out_ref):
    out_ref[0] = (
        jnp.dot(silu_ref[...], w_ref[0], preferred_element_type=f32) + b_ref[0]
    )


def modes_call(silu_low, w_mod, b_mod):
    slots, width = silu_low.shape
    local = w_mod.shape[2]
    return pl.pallas_call(
        modes_kernel,
        grid=(6,),
        in_specs=[
            spec((slots, width), lambda g: (0, 0)),
            spec((1, width, local), lambda g: (g, 0, 0)),
            spec((1, 1, local), lambda g: (g, 0, 0)),
        ],
        out_specs=spec((1, slots, local), lambda g: (g, 0, 0)),
        out_shape=jax.ShapeDtypeStruct((6, slots, local), f32),
        compiler_params=params(),
        name="modes",
    )(silu_low, w_mod, b_mod[:, None, :])


def silu_back_kernel(d_ref, w_ref, out_ref):
    part = dot(d_ref[0], w_ref[0], ((1,), (1,)))

    @pl.when(pl.program_id(0) == 0)
    def _():
        out_ref[...] = part

    @pl.when(pl.program_id(0) > 0)
    def _():
        out_ref[...] = out_ref[...] + part


def silu_back_call(d_modes, w_mod):
    groups, slots, local = d_modes.shape
    width = w_mod.shape[1]
    return pl.pallas_call(
        silu_back_kernel,
        grid=(groups,),
        in_specs=[
            spec((1, slots, local), lambda g: (g, 0, 0)),
            spec((1, width, local), lambda g: (g, 0, 0)),
        ],
        out_specs=spec((slots, width), lambda g: (0, 0)),
        out_shape=jax.ShapeDtypeStruct((slots, width), f32),
        compiler_params=params(),
        name="silu_back",
    )(d_modes, w_mod)


def mix_kernel(order_ref, slot_ref, tok_ref, shift_ref, scale_ref, out_ref):
    step = pl.program_id(0)
    spans = tok_ref.shape[0] // SPAN
    for i in range(spans):
        rows = slice(i * SPAN, (i + 1) * SPAN)
        slot = slot_ref[step * spans + i]
        values = tok_ref[rows, :].astype(f32)
        centred = values - jnp.mean(values, axis=-1, keepdims=True)
        recip = lax.rsqrt(jnp.mean(centred * centred, axis=-1, keepdims=True) + 1e-06)
        shift = shift_ref[0, pl.ds(slot, 1), :]
        scale = scale_ref[0, pl.ds(slot, 1), :]
        out_ref[rows, :] = (centred * recip * (1.0 + scale) + shift).astype(half)


def gate_kernel(order_ref, slot_ref, grad_ref, gate_ref, out_ref):
    step = pl.program_id(0)
    spans = grad_ref.shape[0] // SPAN
    for i in range(spans):
        rows = slice(i * SPAN, (i + 1) * SPAN)
        gate = gate_ref[0, pl.ds(slot_ref[step * spans + i], 1), :]
        out_ref[rows, :] = (grad_ref[rows, :].astype(f32) * gate).astype(half)


def by_chunk(kernel, name, order, slots, values, modes, columns):
    rows, width = values.shape
    chunk = rows // order.shape[0]
    count = modes.shape[1]
    mode_specs = [
        spec((1, count, width), lambda i, o, s, column=column: (column, 0, 0)) for column in columns
    ]
    return pl.pallas_call(
        kernel,
        grid_spec=pltpu.PrefetchScalarGridSpec(
            num_scalar_prefetch=2,
            grid=(order.shape[0],),
            in_specs=[spec((chunk, width), lambda i, o, s: (o[i], 0))] + mode_specs,
            out_specs=spec((chunk, width), lambda i, o, s: (i, 0)),
        ),
        out_shape=jax.ShapeDtypeStruct((rows, width), half),
        compiler_params=params(),
        name=name,
    )(order, slots, values, *([modes] * len(columns)))


def attend_kernel(q_ref, k_ref, v_ref, qcode_ref, kcode_ref, out_ref, lse_ref):
    heads = q_ref.shape[1] // HEAD_DIM
    for h in range(heads):
        cols = slice(h * HEAD_DIM, (h + 1) * HEAD_DIM)
        keys = jnp.concatenate([k_ref[:, cols], kcode_ref[...]], axis=1)
        query = jnp.concatenate([q_ref[:, cols], qcode_ref[...]], axis=1)
        scores = dot(keys, query, ((1,), (1,)))
        top = jnp.max(scores, axis=0, keepdims=True)
        expo = jnp.exp(scores - top)
        total = jnp.sum(expo, axis=0, keepdims=True)
        out = dot(v_ref[:, cols], expo.astype(half), ((0,), (0,)))
        out_ref[:, cols] = (out / total).T.astype(half)
        lse_ref[0, h : h + 1, :] = top + jnp.log(total)


def attend_call(query, keys, values, qcode, kcode, chunks):
    rows, local = query.shape
    chunk = rows // chunks
    heads = local // HEAD_DIM
    whole = lambda i: (0, 0)
    part = lambda i: (i, 0)
    return pl.pallas_call(
        attend_kernel,
        grid=(chunks,),
        in_specs=[
            spec((chunk, local), part),
            spec((rows, local), whole),
            spec((rows, local), whole),
            spec((chunk, HEAD_DIM), part),
            spec((rows, HEAD_DIM), whole),
        ],
        out_specs=[spec((chunk, local), part), spec((1, heads, chunk), lambda i: (i, 0, 0))],
        out_shape=[
            jax.ShapeDtypeStruct((rows, local), half),
            jax.ShapeDtypeStruct((chunks, heads, chunk), f32),
        ],
        compiler_params=params(),
        cost_estimate=pl.CostEstimate(
            flops=6 * rows * rows * local, transcendentals=rows * rows * heads, bytes_accessed=8 * rows * local
        ),
        name="attend",
    )(query, keys, values, qcode, kcode)


def attend_back_kernel(q_ref, k_ref, v_ref, qcode_ref, kcode_ref, d_ref, lse_ref, dq_ref, dk_ref, dv_ref, dk_acc, dv_acc):
    heads = q_ref.shape[1] // HEAD_DIM
    step = pl.program_id(0)
    factor = HEAD_DIM ** (-0.5)

    @pl.when(step == 0)
    def _():
        dk_acc[...] = jnp.zeros_like(dk_acc)
        dv_acc[...] = jnp.zeros_like(dv_acc)

    for h in range(heads):
        cols = slice(h * HEAD_DIM, (h + 1) * HEAD_DIM)
        keys = jnp.concatenate([k_ref[:, cols], kcode_ref[...]], axis=1)
        query = jnp.concatenate([q_ref[:, cols], qcode_ref[...]], axis=1)
        grad = d_ref[:, cols]
        scores = dot(keys, query, ((1,), (1,)))
        probs = jnp.exp(scores - lse_ref[0, h : h + 1, :])
        d_probs = dot(v_ref[:, cols], grad, ((1,), (1,)))
        inner = jnp.sum(probs * d_probs, axis=0, keepdims=True)
        d_scores = (probs * (d_probs - inner)).astype(half)
        dv_acc[:, cols] += dot(probs.astype(half), grad, ((1,), (0,)))
        dk_acc[:, cols] += dot(d_scores, q_ref[:, cols], ((1,), (0,)))
        dq = dot(k_ref[:, cols], d_scores, ((0,), (0,)))
        dq_ref[:, cols] = (dq.T * factor).astype(half)

    @pl.when(step == pl.num_programs(0) - 1)
    def _():
        dk_ref[...] = dk_acc[...].astype(half)
        dv_ref[...] = dv_acc[...].astype(half)


def attend_back_call(query, keys, values, qcode, kcode, d_heads, lse):
    rows, local = query.shape
    chunks, heads, chunk = lse.shape
    whole = lambda i: (0, 0)
    part = lambda i: (i, 0)
    shape = jax.ShapeDtypeStruct((rows, local), half)
    return pl.pallas_call(
        attend_back_kernel,
        grid=(chunks,),
        in_specs=[
            spec((chunk, local), part),
            spec((rows, local), whole),
            spec((rows, local), whole),
            spec((chunk, HEAD_DIM), part),
            spec((rows, HEAD_DIM), whole),
            spec((chunk, local), part),
            spec((1, heads, chunk), lambda i: (i, 0, 0)),
        ],
        out_specs=[spec((chunk, local), part), spec((rows, local), whole), spec((rows, local), whole)],
        out_shape=[shape, shape, shape],
        scratch_shapes=[pltpu.VMEM((rows, local), f32), pltpu.VMEM((rows, local), f32)],
        compiler_params=params(),
        cost_estimate=pl.CostEstimate(
            flops=14 * rows * rows * local, transcendentals=rows * rows * heads, bytes_accessed=16 * rows * local
        ),
        name="attend_back",
    )(query, keys, values, qcode, kcode, d_heads, lse)


def mlp_kernel(x_ref, up_ref, b_ref, d_ref, hidden_ref, d_pre_ref, dx_ref, acc_ref):
    step = pl.program_id(0)
    pre = jnp.dot(x_ref[...], up_ref[...], preferred_element_type=f32) + b_ref[...]
    cumul = 0.5 * (1.0 + lax.erf(pre * 0.7071067811865476))
    density = jnp.exp(-0.5 * pre * pre) * 0.3989422804014327
    hidden_ref[...] = (pre * cumul).astype(half)
    d_pre = (d_ref[...].astype(f32) * (cumul + pre * density)).astype(half)
    d_pre_ref[...] = d_pre
    part = dot(d_pre, up_ref[...], ((1,), (1,)))

    @pl.when(step == 0)
    def _():
        acc_ref[...] = part

    @pl.when(step > 0)
    def _():
        acc_ref[...] += part

    @pl.when(step == pl.num_programs(0) - 1)
    def _():
        dx_ref[...] = acc_ref[...].astype(half)


def mlp_call(mixed, w_up, b_up, d_hidden):
    rows, width = mixed.shape
    ff = w_up.shape[1]
    block = min(512, ff)
    return pl.pallas_call(
        mlp_kernel,
        grid=(ff // block,),
        in_specs=[
            spec((rows, width), lambda j: (0, 0)),
            spec((width, block), lambda j: (0, j)),
            spec((1, block), lambda j: (0, j)),
            spec((rows, block), lambda j: (0, j)),
        ],
        out_specs=[
            spec((rows, block), lambda j: (0, j)),
            spec((rows, block), lambda j: (0, j)),
            spec((rows, width), lambda j: (0, 0)),
        ],
        out_shape=[
            jax.ShapeDtypeStruct((rows, ff), half),
            jax.ShapeDtypeStruct((rows, ff), half),
            jax.ShapeDtypeStruct((rows, width), half),
        ],
        scratch_shapes=[pltpu.VMEM((rows, width), f32)],
        compiler_params=params(),
        cost_estimate=pl.CostEstimate(
            flops=4 * rows * width * ff, transcendentals=rows * ff, bytes_accessed=2 * width * ff + 6 * rows * ff
        ),
        name="mlp",
    )(mixed, w_up, b_up[None, :], d_hidden)


def normalize(values):
    centred = values - jnp.mean(values, axis=-1, keepdims=True)
    recip = lax.rsqrt(jnp.mean(centred * centred, axis=-1, keepdims=True) + 1e-06)
    return (centred * recip, recip)


def norm_back(grad, normed, recip):
    first = jnp.mean(grad, axis=-1, keepdims=True)
    second = jnp.mean(grad * normed, axis=-1, keepdims=True)
    return recip * (grad - first - normed * second)


def after(values, *others):
    return lax.optimization_barrier((values, *others))[0]


def make_body(n_wide, n_narrow):
    def body(
        tokens,
        cotangent,
        noise_emb,
        offsets,
        lengths,
        group_ids,
        group_table,
        w_qkv,
        w_out,
        w_up,
        b_up,
        w_down,
        w_mod,
        b_mod,
    ):
        tok_dev, width = tokens.shape
        slots = offsets.shape[1]
        local = w_qkv.shape[2]
        groups = group_table.shape[0]
        rows = tok_dev // n_narrow
        spans = rows // SPAN
        me = lax.axis_index("narrow")
        place = lax.axis_index("wide")
        order = me ^ jnp.arange(n_narrow, dtype=jnp.int32)

        starts = (order[:, None] * spans + jnp.arange(spans, dtype=jnp.int32)[None, :]).reshape(-1, 1) * SPAN
        inside = (starts >= offsets) & (starts < offsets + lengths)
        slot_hot = inside.astype(f32)
        slot_of = jnp.sum(inside * jnp.arange(slots, dtype=jnp.int32)[None, :], axis=1).astype(jnp.int32)
        lanes = jnp.arange(HEAD_DIM, dtype=jnp.int32)
        same = jnp.repeat(slot_of, SPAN)[:, None] == lanes[None, :]
        kcode = same.astype(half)
        qcode = jnp.where(same, 0.0, MASKED).astype(half)

        group_hot = (group_ids[0][:, None] == jnp.arange(groups, dtype=jnp.int32)[None, :]).astype(f32)
        cond = noise_emb + jnp.dot(group_hot, group_table, precision=highest)
        silu_low = jax.nn.silu(cond).astype(half)
        w_mod_t = w_mod.transpose(1, 0, 2)
        modes_own = modes_call(silu_low, w_mod_t, b_mod)
        modes = in_order([modes_own] + [hop(modes_own, d, n_narrow) for d in range(1, n_narrow)], me, 2)

        mixed_a = by_chunk(mix_kernel, "mix_a", order, slot_of, tokens, modes, (0, 1))
        factor = HEAD_DIM ** (-0.5)
        query = (jnp.dot(mixed_a, w_qkv[0], preferred_element_type=f32) * factor).astype(half)
        keys = jnp.dot(mixed_a, w_qkv[1], preferred_element_type=f32).astype(half)
        values = jnp.dot(mixed_a, w_qkv[2], preferred_element_type=f32).astype(half)
        heads_out, lse = attend_call(query, keys, values, qcode, kcode, n_narrow)

        def chunk(array, d):
            return array[d * rows : (d + 1) * rows]

        sent = [
            jnp.dot(chunk(heads_out, d), w_out, preferred_element_type=f32).astype(half if d else f32)
            for d in range(n_narrow)
        ]
        attended = collect(sent, n_narrow)

        mine = jnp.einsum("bs,gsv->gbv", slot_hot[:spans], modes, precision=highest)

        def per_token(column):
            return jnp.broadcast_to(mine[column][:, None, :], (spans, SPAN, width)).reshape(rows, width)

        tok_own = lax.dynamic_slice_in_dim(tokens, me * rows, rows, 0).astype(f32)
        grad_own = lax.dynamic_slice_in_dim(cotangent, me * rows, rows, 0).astype(f32)
        middle = tok_own + per_token(2) * attended
        normed_b, recip_b = normalize(middle)
        mixed_own = (normed_b * (1.0 + per_token(4)) + per_token(3)).astype(half)
        mixed_b = spread(mixed_own, n_narrow)

        d_mlp = by_chunk(gate_kernel, "d_mlp", order, slot_of, cotangent, modes, (5,))
        d_hidden = dot(d_mlp, w_down, ((1,), (1,))).astype(half)
        hidden, d_pre, d_mixed = [], [], []
        for d in range(n_narrow):
            outs = mlp_call(mixed_b[d], w_up, b_up, chunk(d_hidden, d))
            hidden.append(outs[0])
            d_pre.append(outs[1])
            d_mixed.append(outs[2])
        d_mixed_b = collect(d_mixed, n_narrow)

        d_middle = grad_own + norm_back(d_mixed_b * (1.0 + per_token(4)), normed_b, recip_b)
        d_attn_own = (d_middle * per_token(2)).astype(half)
        d_attn = jnp.concatenate(spread(d_attn_own, n_narrow), axis=0)

        hidden = jnp.concatenate(hidden, axis=0)
        d_pre = jnp.concatenate(d_pre, axis=0)
        mixed_b = jnp.concatenate(mixed_b, axis=0)
        grad_b_up = jnp.sum(d_pre.astype(f32), axis=0)
        grad_w_down = dot(d_mlp, hidden, ((0,), (0,))).astype(half)
        grad_w_up = dot(mixed_b, d_pre, ((0,), (0,))).astype(half)
        sum_w_down = lax.psum_scatter(grad_w_down, "wide", scatter_dimension=0, tiled=True)
        sum_w_up = lax.psum_scatter(grad_w_up, "wide", scatter_dimension=0, tiled=True)

        mlp_sent = [
            jnp.dot(chunk(hidden, d), w_down, preferred_element_type=f32).astype(half if d else f32)
            for d in range(n_narrow)
        ]
        mlp_out = collect(mlp_sent, n_narrow)
        result_own = (middle + per_token(5) * mlp_out).astype(half)
        result = in_order(spread(result_own, n_narrow), me)

        d_heads = dot(d_attn, w_out, ((1,), (1,))).astype(half)
        grad_w_out = dot(d_attn, heads_out, ((0,), (0,))).astype(half)
        sum_w_out = lax.psum_scatter(grad_w_out, "wide", scatter_dimension=0, tiled=True)
        d_query, d_key, d_value = attend_back_call(query, keys, values, qcode, kcode, d_heads, lse)
        d_proj = jnp.concatenate([d_query, d_key, d_value], axis=1)
        w_flat = jnp.concatenate([w_qkv[0], w_qkv[1], w_qkv[2]], axis=1)
        sent_a = [
            dot(chunk(d_proj, d), w_flat, ((1,), (1,))).astype(half if d else f32) for d in range(n_narrow)
        ]
        d_mixed_a = collect(sent_a, n_narrow)
        grad_w_qkv = dot(mixed_a, d_proj, ((0,), (0,))).astype(half)
        sum_w_qkv = lax.psum_scatter(grad_w_qkv, "wide", scatter_dimension=0, tiled=True)

        normed_a, recip_a = normalize(tok_own)
        grad_tok_own = (d_middle + norm_back(d_mixed_a * (1.0 + per_token(1)), normed_a, recip_a)).astype(half)
        grad_tokens = in_order(spread(grad_tok_own, n_narrow), me)

        def span_sums(terms):
            return jnp.sum(terms.reshape(spans, SPAN, width), axis=1)

        sums = jnp.stack(
            [
                span_sums(d_mixed_a),
                span_sums(d_mixed_a * normed_a),
                span_sums(d_middle * attended),
                span_sums(d_mixed_b),
                span_sums(d_mixed_b * normed_b),
                span_sums(grad_own * mlp_out),
            ]
        )
        pieces = [
            hop(lax.dynamic_slice_in_dim(sums, (me ^ d) * local, local, 2), d, n_narrow) if d else
            lax.dynamic_slice_in_dim(sums, me * local, local, 2)
            for d in range(n_narrow)
        ]
        d_modes = jnp.einsum(
            "bs,gbv->gsv", slot_hot, jnp.concatenate(pieces, axis=1), precision=highest
        ).astype(half)
        d_silu_part = silu_back_call(d_modes, w_mod_t).astype(half)
        d_silu = d_silu_part.astype(f32)
        for d in range(1, n_narrow):
            d_silu = d_silu + hop(d_silu_part, d, n_narrow).astype(f32)
        sigma = jax.nn.sigmoid(cond)
        grad_noise = d_silu * sigma * (1.0 + cond * (1.0 - sigma))
        table_part = jnp.dot(group_hot.T, grad_noise, precision=highest).astype(half)

        col = width // n_wide
        silu_all = lax.all_gather(silu_low, "wide", axis=0, tiled=True)
        silu_cols = lax.dynamic_slice_in_dim(silu_all, place * col, col, 1)
        b_up_all = lax.all_gather(grad_b_up.astype(half), "wide", axis=0)
        ff_part = b_up_all.shape[1] // n_wide
        sum_b_up = jnp.sum(
            lax.dynamic_slice_in_dim(b_up_all, place * ff_part, ff_part, 1).astype(f32), axis=0
        )
        d_modes_all = lax.all_gather(d_modes, "wide", axis=1, tiled=True)
        grad_w_mod = jnp.einsum("sd,gsv->gdv", silu_cols, d_modes_all, preferred_element_type=f32).transpose(1, 0, 2)
        part_b = local // n_wide
        sum_b_mod = jnp.sum(
            lax.dynamic_slice_in_dim(d_modes_all, place * part_b, part_b, 2).astype(f32), axis=1
        )
        table_all = lax.all_gather(table_part, "wide", axis=0)
        sum_table = jnp.sum(lax.dynamic_slice_in_dim(table_all, place * col, col, 2).astype(f32), axis=0)

        out_qkv = sum_w_qkv.astype(f32).reshape(col, 3, local).transpose(1, 0, 2)
        return (
            result,
            grad_tokens,
            grad_noise,
            sum_table,
            out_qkv,
            sum_w_out.astype(f32).T,
            sum_w_up.astype(f32),
            sum_b_up,
            sum_w_down.astype(f32).T,
            grad_w_mod,
            sum_b_mod,
        )

    return body


def solution(mesh):
    in_specs = (
        P("wide", None),
        P("wide", None),
        P("wide", None),
        P("wide", None),
        P("wide", None),
        P("wide", None),
        P(),
        P(None, None, "narrow"),
        P("narrow", None),
        P(None, "narrow"),
        P("narrow"),
        P("narrow", None),
        P(None, None, "narrow"),
        P(None, "narrow"),
    )
    out_specs = (
        P("wide", None),
        P("wide", None),
        P("wide", None),
        P(None, "wide"),
        P(None, "wide", "narrow"),
        P("narrow", "wide"),
        P("wide", "narrow"),
        P(("narrow", "wide")),
        P("narrow", "wide"),
        P("wide", None, "narrow"),
        P(None, ("narrow", "wide")),
    )
    body = make_body(mesh.shape["wide"], mesh.shape["narrow"])
    return jax.shard_map(body, mesh=mesh, in_specs=in_specs, out_specs=out_specs, check_vma=False)
```

time: 1390 us -> 636 us (0.46)
  waiting for transfers between devices: 897 us -> 181 us
  matrix products: 258 us -> 118 us
  Pallas kernels: 0 us -> 103 us
  other arithmetic: 126 us -> 40 us
  starting transfers between devices: 0.46 us -> 47.2 us
  blocking collectives: 31.3 us -> 68 us
    psum x4 -> x0, waiting for transfers between devices: 490 us -> none  [the longest x1 166 us: body(): lax.psum(jnp.dot(hidden, w_down, preferred_element_type=f32).astype(jnp.b...]
    reduce_scatter x5 -> x4, waiting for transfers between devices: 372 us -> 41 us  [the longest x1 41 us: body(): lax.psum_scatter(grad_w_up, 'wide', scatter_dimension=0, tiled=True)]
    dot_general x37 -> x22, matrix products: 248 us -> 103 us  [the longest x10 64.7 us: dot(): lax.dot_general(left, right, (dims, ((), ())), preferred_element_type=f32)]
    ppermute x0 -> x41, waiting for transfers between devices: none -> 140 us  [hop(): lax.ppermute(values, 'narrow', [(i, i ^ distance) for i in range(size)])]
    pallas_call x0 -> x10, Pallas kernels: none -> 103 us  [the longest x4 41.8 us: mlp_call(): pl.pallas_call(mlp_kernel, grid=(ff // block,), in_specs=[spec((rows, wid...]
    convert_element_type x18 -> x12, other arithmetic: 74.9 us -> 6.5 us  [the longest x1 2.79 us: body(): sum_w_up.astype(f32)]
    all_gather x1 -> x4, blocking collectives: 15.2 us -> 68 us  [the longest x1 19.8 us: body(): d_modes_all = lax.all_gather(d_modes, 'wide', axis=1, tiled=True)]
    ppermute x0 -> x41, starting transfers between devices: none -> 46.8 us  [hop(): lax.ppermute(values, 'narrow', [(i, i ^ distance) for i in range(size)])]
  transfers between devices with their start and end apart: 11 -> 45, of which waited for: 10 -> 20; matrix products, arithmetic and copies ran while one was open for 9% -> 23% of each run, Pallas kernels for 0% -> 10%
where the time goes in v1:
time: 636 us; the launch traced here: 626 us
  waiting for transfers between devices  181 us (28%)
  matrix products  118 us (19%)
  Pallas kernels  103 us (16%)
  blocking collectives  68 us (11%)
  local copies, waits for them, and re-layouts  53.7 us (8%)
  starting transfers between devices  47.2 us (7%)
  other arithmetic  40 us (6%)
  between operations  14.9 us (2%)
    ppermute x41, waiting for transfers between devices, hop(): lax.ppermute(values, 'narrow', [(i, i ^ distance) for i in range(size)])  140 us
    dot_general x10, matrix products, dot(): lax.dot_general(left, right, (dims, ((), ())), preferred_element_type=f32)  64.7 us
    ppermute x41, starting transfers between devices, hop(): lax.ppermute(values, 'narrow', [(i, i ^ distance) for i in range(size)])  46.8 us
    pallas_call x4, Pallas kernels, mlp_call(): pl.pallas_call(mlp_kernel, grid=(ff // block,), in_specs=[spec((rows, wid...  41.8 us
    reduce_scatter x1, waiting for transfers between devices, body(): lax.psum_scatter(grad_w_up, 'wide', scatter_dimension=0, tiled=True)  41 us
    unnamed x136, local copies, waits for them, and re-layouts  28.6 us
    dot_general x4, matrix products, body(): jnp.dot(chunk(hidden, d), w_down, preferred_element_type=f32)  28.2 us
    all_gather x1, blocking collectives, body(): d_modes_all = lax.all_gather(d_modes, 'wide', axis=1, tiled=True)  19.8 us
  transfers between devices with their start and end apart: 45, of which 20 were waited for; matrix products, arithmetic and copies ran while one was open for 23% of the time, Pallas kernels for 10%

profile of v1, /device:TPU:0, one launch (start us, length us, event | category | flops | bytes accessed | tf_op | source)
XLA Modules:
  0.0 626.2 jit_solution(14823253573975540473)
XLA Ops:
  52.9 13.0 %attend.1 = (bf16[1024,512]{1,0:T(8,128)(2,1)}, f32[4,4,256]{2,1,0:T(4,128)}) custom-call(bf16[1024,512]{1,0:T(8,128)(2,1)} %multiply_convert_fusion.q_ref, bf16[1024,512]{1,0:T(8,128)(2,1)} %convolution_convert_fusion.17.k_ref, bf16[1024,512]{1,0:T(8,128)(2,1)} %convolution_convert_fusion.16.v_ref, bf16[1024,128]{1,0:T(8,128)(2,1)} %select_convert_fusion.qcode_ref, ...), custom_call_target="tpu_custom_call" | custom-call | flops 3221225472 | bytes 4194304 | tf_op jit(solution)/shard_map/attend/pallas_call | solution.py:194
  71.6 8.8 %collective-permute-done.3 = bf16[128,2048]{1,0:T(8,128)(2,1)S(1)} collective-permute-done((bf16[128,2048]{1,0:T(8,128)(2,1)S(1)}, bf16[128,2048]{1,0:T(8,128)(2,1)S(1)}, u32[]{:S(2)}, u32[]{:S(2)}) %collective-permute-start.3) | collective-permute-done | bytes 524320 | tf_op jit(solution)/shard_map/ppermute | solution.py:31
  92.1 11.9 %collective-permute-done.4 = bf16[256,2048]{1,0:T(8,128)(2,1)S(1)} collective-permute-done((bf16[256,2048]{1,0:T(8,128)(2,1)S(1)}, bf16[256,2048]{1,0:T(8,128)(2,1)S(1)}, u32[]{:S(2)}, u32[]{:S(2)}) %collective-permute-start.4) | collective-permute-done | bytes 1048608 | tf_op jit(solution)/shard_map/ppermute | solution.py:31
  113.4 11.3 %convolution_convert_fusion.3 = bf16[1024,2048]{1,0:T(8,128)(2,1)S(1)} fusion(bf16[1024,2048]{1,0:T(8,128)(2,1)S(1)} %copy-done.11, bf16[2048,2048]{1,0:T(8,128)(2,1)} %param.25), kind=kOutput, calls=%fused_computation.18 | convolution fusion | flops 8592031744 | bytes 16777216 | tf_op jit(solution)/shard_map/dot_general | solution.py:19
  139.7 10.4 %mlp.5 = (bf16[256,2048]{1,0:T(8,128)(2,1)}, bf16[256,2048]{1,0:T(8,128)(2,1)}, bf16[256,2048]{1,0:T(8,128)(2,1)}) custom-call(bf16[256,2048]{1,0:T(8,128)(2,1)} %copy-done.14, bf16[2048,2048]{1,0:T(8,128)(2,1)} %up_ref.7, f32[1,2048]{1,0:T(1,128)} %bitcast.148, bf16[256,2048]{1,0:T(8,128)(2,1)} %get-tuple-element.109.d_ref), custom_call_target="tpu_custom_call" | custom-call | flops 4294967296 | bytes 11534336 | tf_op jit(solution)/shard_map/mlp/pallas_call | solution.py:304
  157.1 10.7 %mlp.7 = (bf16[256,2048]{1,0:T(8,128)(2,1)}, bf16[256,2048]{1,0:T(8,128)(2,1)}, bf16[256,2048]{1,0:T(8,128)(2,1)}) custom-call(bf16[256,2048]{1,0:T(8,128)(2,1)} %copy-done.16, bf16[2048,2048]{1,0:T(8,128)(2,1)} %up_ref.7, f32[1,2048]{1,0:T(1,128)} %bitcast.149, bf16[256,2048]{1,0:T(8,128)(2,1)} %get-tuple-element.110.d_ref), custom_call_target="tpu_custom_call" | custom-call | flops 4294967296 | bytes 11534336 | tf_op jit(solution)/shard_map/mlp/pallas_call | solution.py:304
  169.9 10.3 %mlp.6 = (bf16[256,2048]{1,0:T(8,128)(2,1)}, bf16[256,2048]{1,0:T(8,128)(2,1)}, bf16[256,2048]{1,0:T(8,128)(2,1)}) custom-call(bf16[256,2048]{1,0:T(8,128)(2,1)} %pad_maximum_fusion.3.x_ref, bf16[2048,2048]{1,0:T(8,128)(2,1)} %up_ref.7, f32[1,2048]{1,0:T(1,128)} %bitcast.150, bf16[256,2048]{1,0:T(8,128)(2,1)} %get-tuple-element.111.d_ref), custom_call_target="tpu_custom_call" | custom-call | flops 4294967296 | bytes 11534336 | tf_op jit(solution)/shard_map/mlp/pallas_call | solution.py:304
  199.9 9.9 %collective-permute-done.13 = bf16[128,2048]{1,0:T(8,128)(2,1)S(1)} collective-permute-done((bf16[128,2048]{1,0:T(8,128)(2,1)S(1)}, bf16[128,2048]{1,0:T(8,128)(2,1)S(1)}, u32[]{:S(2)}, u32[]{:S(2)}) %collective-permute-start.13) | collective-permute-done | bytes 524320 | tf_op jit(solution)/shard_map/ppermute | solution.py:31
  223.3 10.4 %mlp.4 = (bf16[256,2048]{1,0:T(8,128)(2,1)}, bf16[256,2048]{1,0:T(8,128)(2,1)}, bf16[256,2048]{1,0:T(8,128)(2,1)}) custom-call(bf16[256,2048]{1,0:T(8,128)(2,1)} %copy-done.33, bf16[2048,2048]{1,0:T(8,128)(2,1)} %up_ref.7, f32[1,2048]{1,0:T(1,128)} %bitcast.151, bf16[256,2048]{1,0:T(8,128)(2,1)} %get-tuple-element.112.d_ref), custom_call_target="tpu_custom_call" | custom-call | flops 4294967296 | bytes 11534336 | tf_op jit(solution)/shard_map/mlp/pallas_call | solution.py:304
  233.7 9.9 %collective-permute-done.12 = bf16[256,2048]{1,0:T(8,128)(2,1)} collective-permute-done((bf16[256,2048]{1,0:T(8,128)(2,1)}, bf16[256,2048]{1,0:T(8,128)(2,1)}, u32[]{:S(2)}, u32[]{:S(2)}) %collective-permute-start.12) | collective-permute-done | bytes 1048608 | tf_op jit(solution)/shard_map/ppermute | solution.py:31
  243.6 17.5 %collective-permute-done.20 = bf16[256,2048]{1,0:T(8,128)(2,1)} collective-permute-done((bf16[256,2048]{1,0:T(8,128)(2,1)}, bf16[256,2048]{1,0:T(8,128)(2,1)}, u32[]{:S(2)}, u32[]{:S(2)}) %collective-permute-start.20) | collective-permute-done | bytes 1048608 | tf_op jit(solution)/shard_map/ppermute | solution.py:31
  261.2 9.4 %fusion.32 = (f32[256]{0:T(256)S(1)}, f32[256]{0:T(256)S(1)}, bf16[256,2048]{1,0:T(8,128)(2,1)}, f32[256,2048]{1,0:T(8,128)S(1)}) fusion(f32[4,2048]{1,0:T(4,128)S(1)} %get-tuple-element.128, bf16[256,2048]{1,0:T(8,128)(2,1)} %collective-permute-done.22, bf16[256,2048]{1,0:T(8,128)(2,1)} %collective-permute-done.20, ...), kind=kOutput, calls=%fused_computation.79 | convolution fusion | flops 2156920320 | bytes 19992576 | tf_op jit(solution)/shard_map/dot_general | solution.py:443
  277.8 20.9 %collective-permute-done.24 = bf16[256,2048]{1,0:T(8,128)(2,1)S(1)} collective-permute-done((bf16[256,2048]{1,0:T(8,128)(2,1)S(1)}, bf16[256,2048]{1,0:T(8,128)(2,1)S(1)}, u32[]{:S(2)}, u32[]{:S(2)}) %collective-permute-start.24) | collective-permute-done | bytes 1048608 | tf_op jit(solution)/shard_map/ppermute | solution.py:31
  321.8 18.4 %attend_back.1 = (bf16[1024,512]{1,0:T(8,128)(2,1)}, bf16[1024,512]{1,0:T(8,128)(2,1)}, bf16[1024,512]{1,0:T(8,128)(2,1)}) custom-call(bf16[1024,512]{1,0:T(8,128)(2,1)} %multiply_convert_fusion.q_ref, bf16[1024,512]{1,0:T(8,128)(2,1)} %convolution_convert_fusion.17.k_ref, bf16[1024,512]{1,0:T(8,128)(2,1)} %convolution_convert_fusion.16.v_ref, ...), custom_call_target="tpu_custom_call" | custom-call | flops 7516192768 | bytes 8388608 | tf_op jit(solution)/shard_map/attend_back/pallas_call | solution.py:254
  355.4 13.8 %convolution_convert_fusion = bf16[2048,2048]{1,0:T(8,128)(2,1)} fusion(bf16[1024,2048]{1,0:T(8,128)(2,1)} %d_mlp.1, bf16[256,2048]{1,0:T(8,128)(2,1)} %get-tuple-element.31, bf16[256,2048]{1,0:T(8,128)(2,1)} %get-tuple-element.32, bf16[256,2048]{1,0:T(8,128)(2,1)S(1)} %copy-done.56, bf16[256,2048]{1,0:T(8,128)(2,1)S(1)} %copy-done.23), kind=kOutput, calls=%fused_computation | convolution fusion | flops 8610906112 | bytes 16777216 | tf_op jit(solution)/shard_map/dot_general | solution.py:19
  376.0 13.5 %convolution_convert_fusion.1 = bf16[2048,2048]{1,0:T(8,128)(2,1)} fusion(bf16[1024,2048]{1,0:T(8,128)(2,1)} %constant_dynamic-update-slice_fusion.14, bf16[256,2048]{1,0:T(8,128)(2,1)S(1)} %copy-done.28, bf16[256,2048]{1,0:T(8,128)(2,1)S(1)} %copy-done.27, bf16[256,2048]{1,0:T(8,128)(2,1)S(1)} %copy-done.26, bf16[256,2048]{1,0:T(8,128)(2,1)S(1)} %copy-done.29), kind=kOutput, calls=%fused_computation.1 | convolution fusion | flops 8610906112 | bytes 16777216 | tf_op jit(solution)/shard_map/dot_general | solution.py:19
  399.1 19.2 %all_gather.19 = bf16[128,2048]{1,0:T(8,128)(2,1)} all-gather(bf16[16,2048]{1,0:T(8,128)(2,1)S(1)} %copy-done.42), channel_id=1, replica_groups=mesh['wide'=8,'narrow'=4] {'wide'}, dimensions={0}, use_global_device_ids=true | all-gather | bytes 589824 | tf_op jit(solution)/shard_map/all_gather | solution.py:497
  424.0 14.0 %all-gather.1 = bf16[16384]{0:T(1024)(128)(2,1)S(1)} all-gather(bf16[2048]{0:T(1024)(128)(2,1)S(1)} %add_add_fusion), channel_id=3, replica_groups=mesh['wide'=8,'narrow'=4] {'wide'}, dimensions={0}, use_global_device_ids=true | all-gather | bytes 36864 | tf_op jit(solution)/shard_map/all_gather | solution.py:499
  454.1 14.5 %collective-permute-done.27 = bf16[128,2048]{1,0:T(8,128)(2,1)S(1)} collective-permute-done((bf16[128,2048]{1,0:T(8,128)(2,1)S(1)}, bf16[128,2048]{1,0:T(8,128)(2,1)S(1)}, u32[]{:S(2)}, u32[]{:S(2)}) %collective-permute-start.27) | collective-permute-done | bytes 524320 | tf_op jit(solution)/shard_map/ppermute | solution.py:31
  474.5 18.7 %collective-permute-done.28 = bf16[256,2048]{1,0:T(8,128)(2,1)S(1)} collective-permute-done((bf16[256,2048]{1,0:T(8,128)(2,1)S(1)}, bf16[256,2048]{1,0:T(8,128)(2,1)S(1)}, u32[]{:S(2)}, u32[]{:S(2)}) %collective-permute-start.28) | collective-permute-done | bytes 1048608 | tf_op jit(solution)/shard_map/ppermute | solution.py:31
  505.8 19.8 %all_gather.20 = bf16[6,128,512]{2,1,0:T(8,128)(2,1)S(1)} all-gather(bf16[6,16,512]{2,1,0:T(8,128)(2,1)S(1)} %fusion.34.d_ref), channel_id=1, replica_groups=mesh['wide'=8,'narrow'=4] {'wide'}, dimensions={1}, use_global_device_ids=true | all-gather | bytes 884736 | tf_op jit(solution)/shard_map/all_gather | solution.py:504
  525.7 9.1 %silu_back.1 = f32[16,2048]{1,0:T(8,128)} custom-call(bf16[6,16,512]{2,1,0:T(8,128)(2,1)} %copy-done.38, bf16[6,2048,512]{2,1,0:T(8,128)(2,1)} %bitcast.139), custom_call_target="tpu_custom_call" | custom-call | tf_op jit(solution)/shard_map/silu_back/pallas_call | solution.py:115
  546.1 14.9 %all-gather.2 = bf16[8,3,2048]{2,1,0:T(4,128)(2,1)S(1)} all-gather(bf16[1,3,2048]{2,1,0:T(4,128)(2,1)S(1)} %fusion.19), channel_id=2, replica_groups=mesh['wide'=8,'narrow'=4] {'wide'}, dimensions={0}, use_global_device_ids=true | all-gather | bytes 110592 | tf_op jit(solution)/shard_map/all_gather | solution.py:510
  575.7 41.0 %reduce-scatter.9.cloned.1.call-done = bf16[256,2048]{1,0:T(8,128)(2,1)} async-done(((bf16[2048,2048]{1,0:T(8,128)(2,1)}), bf16[256,2048]{1,0:T(8,128)(2,1)}) %reduce-scatter.9.cloned.1.call-update) | async-done | bytes 1048592 | tf_op jit(solution)/shard_map/reduce_scatter | solution.py:440
  (349 shorter events, 259.7 us)
Async XLA Ops:
  7.2 557.7 %reduce-scatter.7.cloned.1.call-start = ((), (), s32[]{:S(2)}) async-start(), calls=%async_computation.5 | async-start | bytes 2359296 | tf_op jit(solution)/shard_map/reduce_scatter | solution.py:452
  80.6 23.4 %collective-permute-start.4 = (bf16[256,2048]{1,0:T(8,128)(2,1)S(1)}, bf16[256,2048]{1,0:T(8,128)(2,1)S(1)}, u32[]{:S(2)}, u32[]{:S(2)}) collective-permute-start(bf16[256,2048]{1,0:T(8,128)(2,1)S(1)} %pad_maximum_fusion.1), channel_id=1, source_target_pairs={{0,1},{1,0},{2,3},{3,2},{4,5},{5,4},{6,7},{7,6},{8,9},{9,8},{10,11... | collective-permute-start | bytes 3145736 | tf_op jit(solution)/shard_map/ppermute | solution.py:31
  82.4 22.9 %collective-permute-start.6 = (bf16[256,2048]{1,0:T(8,128)(2,1)S(1)}, bf16[256,2048]{1,0:T(8,128)(2,1)S(1)}, u32[]{:S(2)}, u32[]{:S(2)}) collective-permute-start(bf16[256,2048]{1,0:T(8,128)(2,1)S(1)} %pad_maximum_fusion.2), channel_id=1, source_target_pairs={{0,2},{1,3},{2,0},{3,1},{4,6},{5,7},{6,4},{7,5},{8,10},{9,11},{10,... | collective-permute-start | bytes 3145736 | tf_op jit(solution)/shard_map/ppermute | solution.py:31
  111.7 24.7 %collective-permute-start.8 = (bf16[256,2048]{1,0:T(8,128)(2,1)S(1)}, bf16[256,2048]{1,0:T(8,128)(2,1)S(1)}, u32[]{:S(2)}, u32[]{:S(2)}) collective-permute-start(bf16[256,2048]{1,0:T(8,128)(2,1)S(1)} %get-tuple-element.140.x_ref), channel_id=1, source_target_pairs={{0,2},{1,3},{2,0},{3,1},{4,6},{5,7},{6,4},{7,5},{8,10},{9,11},{10,... | collective-permute-start | bytes 3145736 | tf_op jit(solution)/shard_map/ppermute | solution.py:31
  134.4 33.4 %collective-permute-start.10 = (bf16[128,2048]{1,0:T(8,128)(2,1)}, bf16[128,2048]{1,0:T(8,128)(2,1)S(1)}, u32[]{:S(2)}, u32[]{:S(2)}) collective-permute-start(bf16[128,2048]{1,0:T(8,128)(2,1)} %slice.232), channel_id=1, source_target_pairs={{0,2},{1,3},{2,0},{3,1},{4,6},{5,7},{6,4},{7,5},{8,10},{9,11},{10,... | collective-permute-start | bytes 1572872 | tf_op jit(solution)/shard_map/ppermute | solution.py:31
  138.2 29.6 %collective-permute-start.9 = (bf16[128,2048]{1,0:T(8,128)(2,1)}, bf16[128,2048]{1,0:T(8,128)(2,1)}, u32[]{:S(2)}, u32[]{:S(2)}) collective-permute-start(bf16[128,2048]{1,0:T(8,128)(2,1)} %slice.231), channel_id=1, source_target_pairs={{0,1},{1,0},{2,3},{3,2},{4,5},{5,4},{6,7},{7,6},{8,9},{9,8},{10,11... | collective-permute-start | bytes 1572872 | tf_op jit(solution)/shard_map/ppermute | solution.py:31
  196.6 24.5 %collective-permute-start.21 = (bf16[128,2048]{1,0:T(8,128)(2,1)S(1)}, bf16[128,2048]{1,0:T(8,128)(2,1)S(1)}, u32[]{:S(2)}, u32[]{:S(2)}) collective-permute-start(bf16[128,2048]{1,0:T(8,128)(2,1)S(1)} %get-tuple-element.117), channel_id=1, source_target_pairs={{0,1},{1,0},{2,3},{3,2},{4,5},{5,4},{6,7},{7,6},{8,9},{9,8},{10,11... | collective-permute-start | bytes 1572872 | tf_op jit(solution)/shard_map/ppermute | solution.py:31
  199.8 43.8 %collective-permute-start.12 = (bf16[256,2048]{1,0:T(8,128)(2,1)}, bf16[256,2048]{1,0:T(8,128)(2,1)}, u32[]{:S(2)}, u32[]{:S(2)}) collective-permute-start(bf16[256,2048]{1,0:T(8,128)(2,1)} %pad_maximum_fusion.4), channel_id=1, source_target_pairs={{0,1},{1,0},{2,3},{3,2},{4,5},{5,4},{6,7},{7,6},{8,9},{9,8},{10,11... | collective-permute-start | bytes 3145736 | tf_op jit(solution)/shard_map/ppermute | solution.py:31
  211.1 32.5 %collective-permute-start.14 = (bf16[256,2048]{1,0:T(8,128)(2,1)}, bf16[256,2048]{1,0:T(8,128)(2,1)}, u32[]{:S(2)}, u32[]{:S(2)}) collective-permute-start(bf16[256,2048]{1,0:T(8,128)(2,1)} %pad_maximum_fusion.5), channel_id=1, source_target_pairs={{0,2},{1,3},{2,0},{3,1},{4,6},{5,7},{6,4},{7,5},{8,10},{9,11},{10,... | collective-permute-start | bytes 3145736 | tf_op jit(solution)/shard_map/ppermute | solution.py:31
  213.3 47.8 %collective-permute-start.20 = (bf16[256,2048]{1,0:T(8,128)(2,1)}, bf16[256,2048]{1,0:T(8,128)(2,1)}, u32[]{:S(2)}, u32[]{:S(2)}) collective-permute-start(bf16[256,2048]{1,0:T(8,128)(2,1)} %pad_maximum_fusion.6), channel_id=1, source_target_pairs={{0,1},{1,0},{2,3},{3,2},{4,5},{5,4},{6,7},{7,6},{8,9},{9,8},{10,11... | collective-permute-start | bytes 3145736 | tf_op jit(solution)/shard_map/ppermute | solution.py:31
  222.3 38.9 %collective-permute-start.22 = (bf16[256,2048]{1,0:T(8,128)(2,1)}, bf16[256,2048]{1,0:T(8,128)(2,1)}, u32[]{:S(2)}, u32[]{:S(2)}) collective-permute-start(bf16[256,2048]{1,0:T(8,128)(2,1)} %pad_maximum_fusion.7), channel_id=1, source_target_pairs={{0,2},{1,3},{2,0},{3,1},{4,6},{5,7},{6,4},{7,5},{8,10},{9,11},{10,... | collective-permute-start | bytes 3145736 | tf_op jit(solution)/shard_map/ppermute | solution.py:31
  276.4 22.3 %collective-permute-start.24 = (bf16[256,2048]{1,0:T(8,128)(2,1)S(1)}, bf16[256,2048]{1,0:T(8,128)(2,1)S(1)}, u32[]{:S(2)}, u32[]{:S(2)}) collective-permute-start(bf16[256,2048]{1,0:T(8,128)(2,1)S(1)} %get-tuple-element.136), channel_id=1, source_target_pairs={{0,2},{1,3},{2,0},{3,1},{4,6},{5,7},{6,4},{7,5},{8,10},{9,11},{10,... | collective-permute-start | bytes 3145736 | tf_op jit(solution)/shard_map/ppermute | solution.py:31
  277.1 22.8 %collective-permute-start.23 = (bf16[256,2048]{1,0:T(8,128)(2,1)S(1)}, bf16[256,2048]{1,0:T(8,128)(2,1)S(1)}, u32[]{:S(2)}, u32[]{:S(2)}) collective-permute-start(bf16[256,2048]{1,0:T(8,128)(2,1)S(1)} %get-tuple-element.136), channel_id=1, source_target_pairs={{0,1},{1,0},{2,3},{3,2},{4,5},{5,4},{6,7},{7,6},{8,9},{9,8},{10,11... | collective-permute-start | bytes 3145736 | tf_op jit(solution)/shard_map/ppermute | solution.py:31
  316.1 250.7 %reduce-scatter.5.cloned.1.call-start = ((), (), s32[]{:S(2)}) async-start(), calls=%async_computation.4 | async-start | bytes 7077888 | tf_op jit(solution)/shard_map/reduce_scatter | solution.py:461
  353.9 215.9 %reduce-scatter.11.cloned.1.call-start = ((), (), s32[]{:S(2)}) async-start(), calls=%async_computation.7 | async-start | bytes 9437184 | tf_op jit(solution)/shard_map/reduce_scatter | solution.py:439
  369.3 247.3 %reduce-scatter.9.cloned.1.call-start = ((), (), s32[]{:S(2)}) async-start(), calls=%async_computation.6 | async-start | bytes 9437184 | tf_op jit(solution)/shard_map/reduce_scatter | solution.py:440
  390.8 52.6 %collective-permute-start.15 = (bf16[256,2048]{1,0:T(8,128)(2,1)S(1)}, bf16[256,2048]{1,0:T(8,128)(2,1)S(1)}, u32[]{:S(2)}, u32[]{:S(2)}) collective-permute-start(bf16[256,2048]{1,0:T(8,128)(2,1)S(1)} %copy-done.10), channel_id=1, source_target_pairs={{0,1},{1,0},{2,3},{3,2},{4,5},{5,4},{6,7},{7,6},{8,9},{9,8},{10,11... | collective-permute-start | bytes 3145736 | tf_op jit(solution)/shard_map/ppermute | solution.py:31
  391.4 50.9 %collective-permute-start.16 = (bf16[256,2048]{1,0:T(8,128)(2,1)S(1)}, bf16[256,2048]{1,0:T(8,128)(2,1)S(1)}, u32[]{:S(2)}, u32[]{:S(2)}) collective-permute-start(bf16[256,2048]{1,0:T(8,128)(2,1)S(1)} %copy-done.10), channel_id=1, source_target_pairs={{0,2},{1,3},{2,0},{3,1},{4,6},{5,7},{6,4},{7,5},{8,10},{9,11},{10,... | collective-permute-start | bytes 3145736 | tf_op jit(solution)/shard_map/ppermute | solution.py:31
  442.3 29.3 %collective-permute-start.17 = (bf16[128,2048]{1,0:T(8,128)(2,1)S(1)}, bf16[128,2048]{1,0:T(8,128)(2,1)S(1)}, u32[]{:S(2)}, u32[]{:S(2)}) collective-permute-start(bf16[128,2048]{1,0:T(8,128)(2,1)S(1)} %slice.240), channel_id=1, source_target_pairs={{0,1},{1,0},{2,3},{3,2},{4,5},{5,4},{6,7},{7,6},{8,9},{9,8},{10,11... | collective-permute-start | bytes 1572872 | tf_op jit(solution)/shard_map/ppermute | solution.py:31
  443.4 28.2 %collective-permute-start.18 = (bf16[128,2048]{1,0:T(8,128)(2,1)S(1)}, bf16[128,2048]{1,0:T(8,128)(2,1)S(1)}, u32[]{:S(2)}, u32[]{:S(2)}) collective-permute-start(bf16[128,2048]{1,0:T(8,128)(2,1)S(1)} %slice.241), channel_id=1, source_target_pairs={{0,2},{1,3},{2,0},{3,1},{4,6},{5,7},{6,4},{7,5},{8,10},{9,11},{10,... | collective-permute-start | bytes 1572872 | tf_op jit(solution)/shard_map/ppermute | solution.py:31
  468.8 24.4 %collective-permute-start.28 = (bf16[256,2048]{1,0:T(8,128)(2,1)S(1)}, bf16[256,2048]{1,0:T(8,128)(2,1)S(1)}, u32[]{:S(2)}, u32[]{:S(2)}) collective-permute-start(bf16[256,2048]{1,0:T(8,128)(2,1)S(1)} %pad_maximum_fusion.8), channel_id=1, source_target_pairs={{0,1},{1,0},{2,3},{3,2},{4,5},{5,4},{6,7},{7,6},{8,9},{9,8},{10,11... | collective-permute-start | bytes 3145736 | tf_op jit(solution)/shard_map/ppermute | solution.py:31
  470.2 24.1 %collective-permute-start.30 = (bf16[256,2048]{1,0:T(8,128)(2,1)S(1)}, bf16[256,2048]{1,0:T(8,128)(2,1)S(1)}, u32[]{:S(2)}, u32[]{:S(2)}) collective-permute-start(bf16[256,2048]{1,0:T(8,128)(2,1)S(1)} %pad_maximum_fusion.9), channel_id=1, source_target_pairs={{0,2},{1,3},{2,0},{3,1},{4,6},{5,7},{6,4},{7,5},{8,10},{9,11},{10,... | collective-permute-start | bytes 3145736 | tf_op jit(solution)/shard_map/ppermute | solution.py:31
  504.0 41.0 %collective-permute-start.31 = (bf16[256,2048]{1,0:T(8,128)(2,1)S(1)}, bf16[256,2048]{1,0:T(8,128)(2,1)S(1)}, u32[]{:S(2)}, u32[]{:S(2)}) collective-permute-start(bf16[256,2048]{1,0:T(8,128)(2,1)S(1)} %get-tuple-element.138), channel_id=1, source_target_pairs={{0,1},{1,0},{2,3},{3,2},{4,5},{5,4},{6,7},{7,6},{8,9},{9,8},{10,11... | collective-permute-start | bytes 3145736 | tf_op jit(solution)/shard_map/ppermute | solution.py:31
  505.0 38.7 %collective-permute-start.32 = (bf16[256,2048]{1,0:T(8,128)(2,1)S(1)}, bf16[256,2048]{1,0:T(8,128)(2,1)S(1)}, u32[]{:S(2)}, u32[]{:S(2)}) collective-permute-start(bf16[256,2048]{1,0:T(8,128)(2,1)S(1)} %get-tuple-element.138), channel_id=1, source_target_pairs={{0,2},{1,3},{2,0},{3,1},{4,6},{5,7},{6,4},{7,5},{8,10},{9,11},{10,... | collective-permute-start | bytes 3145736 | tf_op jit(solution)/shard_map/ppermute | solution.py:31
  (82 other events, 857.5 us)
Sparse Core Ops, SparseCore 0:
  316.3 36.9 reduce-scatter.6
  355.6 73.7 reduce-scatter.4
  431.6 93.8 reduce-scatter.10
  527.7 88.9 reduce-scatter.8
